TPU v7x, 32 devices: a whole 2x2x4 slice. The times are simulated.
32 devices in a mesh: dp: 8 (over y, x, core), tensor: 4 (over z).
Axes of the slice: x: 2, y: 2, z: 4, core: 2. Of those that a mesh axis runs over, the one named last changes fastest.
Arguments:
- tokens: bfloat16 [8192, 2048], P(('dp', 'tensor')), may hold values from -6 to 6
- norm_attn: bfloat16 [2048], P('dp'), may hold values from 0.5 to 1.5
- w_query: bfloat16 [2048, 2048], P('dp', 'tensor'), may hold values from -0.125 to 0.125
- key_matrix: bfloat16 [2048, 1024], P('dp', 'tensor'), may hold values from -0.125 to 0.125
- value_matrix: bfloat16 [2048, 1024], P('dp', 'tensor'), may hold values from -0.125 to 0.125
- gain_query: bfloat16 [128], P('dp'), may hold values from 0.25 to 1.75
- gain_key: bfloat16 [128], P('dp'), may hold values from 0.25 to 1.75
- w_output: bfloat16 [2048, 2048], P('tensor', 'dp'), may hold values from -0.5 to 0.5
- norm_ffn: bfloat16 [2048], P('dp'), may hold values from 0.5 to 1.5
- w_gate: bfloat16 [2048, 6144], P('dp', 'tensor'), may hold values from -0.125 to 0.125
- w_up: bfloat16 [2048, 6144], P('dp', 'tensor'), may hold values from -0.125 to 0.125
- w_down: bfloat16 [6144, 2048], P('tensor', 'dp'), may hold values from -0.078125 to 0.078125
- cotangent: bfloat16 [8192, 2048], P(('dp', 'tensor')), may hold values from -6 to 6
- lengths: int32 [8], replicated, may hold values from 769 to 1024, as said below
- deal_order: int32 [8], replicated, may hold values from 0 to 7, as said below
Outputs:
- block_out: bfloat16 [8192, 2048], P(('dp', 'tensor'))
- grad_tokens: bfloat16 [8192, 2048], P(('dp', 'tensor'))
- grad_norm_attn: float32 [2048], P('dp')
- grad_query: float32 [2048, 2048], P('dp', 'tensor')
- grad_key: float32 [2048, 1024], P('dp', 'tensor')
- grad_value: float32 [2048, 1024], P('dp', 'tensor')
- grad_gain_query: float32 [128], P('dp')
- grad_gain_key: float32 [128], P('dp')
- grad_output: float32 [2048, 2048], P('tensor', 'dp')
- grad_norm_ffn: float32 [2048], P('dp')
- grad_gate: float32 [2048, 6144], P('dp', 'tensor')
- grad_up: float32 [2048, 6144], P('dp', 'tensor')
- grad_down: float32 [6144, 2048], P('tensor', 'dp')
Inputs may be any that keep to these rules, and one draw needn't show every extreme that they name: Data group g takes sequence deal_order[g]; deal_order is a permutation. `lengths`: one group's sequence fills all 1024 of its rows and another's leaves 256 - 1 rows of padding.
All inputs are finite; a program needn't handle non-finite values.
Results may differ from a plain program's by a relative error of at most 0.023.
Values may be sent and summed in bfloat16 or wider, within the bound.
No kernel may reach another device: no remote copies, remote signals or barrier semaphores. Data moves between devices by JAX's collectives and lax.ppermute only.
A program may use at most 192 MiB of HBM per device.

v0:
```python
import jax
import jax.numpy as jnp
from jax import lax
from jax.sharding import PartitionSpec as P

QUERY_HEADS = 16
KEY_VALUE_HEADS = 8
HEAD_SIZE = 128
norm_eps = 1e-06
rope_base = 1000000.0


def rms_scale(value_vectors):
    return lax.rsqrt(jnp.mean(value_vectors * value_vectors, axis=-1, keepdims=True) + norm_eps)


def rope_tables(position):
    half_dim = HEAD_SIZE // 2
    inverse_freq = rope_base ** (-2.0 * jnp.arange(half_dim, dtype=jnp.float32) / HEAD_SIZE)
    angles = position.astype(jnp.float32)[:, None] * inverse_freq[None, :]
    angles = jnp.concatenate([angles, angles], axis=1)
    return (jnp.cos(angles), jnp.sin(angles))


def rotate_half(value_vectors):
    half_dim = value_vectors.shape[-1] // 2
    return jnp.concatenate([-value_vectors[..., half_dim:], value_vectors[..., :half_dim]], axis=-1)


def rotate_back(value_vectors):
    half_dim = value_vectors.shape[-1] // 2
    return jnp.concatenate([value_vectors[..., half_dim:], -value_vectors[..., :half_dim]], axis=-1)


def group_layout(lengths, deal_order, group_id, count_of_rows):
    slots = jnp.arange(deal_order.shape[0], dtype=jnp.int32)
    seq_taken = jnp.sum(jnp.where(slots == group_id, deal_order, 0))
    seq_len = jnp.sum(jnp.where(slots == seq_taken, lengths, 0))
    row_index = jnp.arange(count_of_rows, dtype=jnp.int32)
    segment = (row_index >= seq_len).astype(jnp.int32)
    seg_start = jnp.where(segment == 0, 0, seq_len)
    return (segment, row_index - seg_start, row_index < seq_len)


def contract_rows(left, right):
    return lax.dot_general(
        left, right, (((0,), (0,)), ((), ())), preferred_element_type=jnp.float32
    )


def times_transpose(left, right):
    return lax.dot_general(
        left, right, (((1,), (1,)), ((), ())), preferred_element_type=jnp.float32
    )


def masked_scores(query_head, key_head, allowed):
    scores = jnp.einsum(
        "qgd,kd->gqk", query_head, key_head, preferred_element_type=jnp.float32
    ) * HEAD_SIZE ** (-0.5)
    return jnp.where(allowed[None], scores, -1e30)


def attend_head(query_head, key_head, value_head, allowed):
    scores = masked_scores(query_head, key_head, allowed)
    top_score = jnp.max(scores, axis=-1, keepdims=True)
    raised = jnp.exp(scores - top_score)
    summed = jnp.sum(raised, axis=-1, keepdims=True)
    attn_probs = (raised / summed).astype(jnp.bfloat16)
    context = jnp.einsum("gqk,kd->qgd", attn_probs, value_head, preferred_element_type=jnp.float32)
    return (context.astype(jnp.bfloat16), top_score[..., 0] + jnp.log(summed[..., 0]))


def attend_back(query_head, key_head, value_head, d_context_head, log_total, allowed):
    scores = masked_scores(query_head, key_head, allowed)
    attn_full = jnp.exp(scores - log_total[..., None])
    attn_probs = attn_full.astype(jnp.bfloat16)
    d_value = jnp.einsum(
        "gqk,qgd->kd", attn_probs, d_context_head, preferred_element_type=jnp.float32
    )
    d_probs = jnp.einsum(
        "qgd,kd->gqk", d_context_head, value_head, preferred_element_type=jnp.float32
    )
    row_dot = jnp.sum(attn_full * d_probs, axis=-1, keepdims=True)
    d_scores = (attn_full * (d_probs - row_dot)).astype(jnp.bfloat16)
    d_query = jnp.einsum(
        "gqk,kd->qgd", d_scores, key_head, preferred_element_type=jnp.float32
    ) * HEAD_SIZE ** (-0.5)
    d_key = jnp.einsum(
        "gqk,qgd->kd", d_scores, query_head, preferred_element_type=jnp.float32
    ) * HEAD_SIZE ** (-0.5)
    return (d_query, d_key, d_value)


def norm_back(d_unit, pre_values, pre_scale, gain_values):
    mixed_terms = gain_values * d_unit
    return pre_scale * mixed_terms - pre_values * pre_scale**3 * jnp.mean(
        mixed_terms * pre_values, axis=-1, keepdims=True
    )


def local(
    tokens,
    norm_attn,
    w_query,
    key_matrix,
    value_matrix,
    gain_query,
    gain_key,
    w_output,
    norm_ffn,
    w_gate,
    w_up,
    w_down,
    cotangent,
    lengths,
    deal_order,
):
    local_rows = tokens.shape[0]
    group_rows = local_rows * lax.axis_size("tensor")
    heads_here = QUERY_HEADS // lax.axis_size("tensor")
    key_value_local = KEY_VALUE_HEADS // lax.axis_size("tensor")
    rows_per_group = QUERY_HEADS // KEY_VALUE_HEADS
    q_width = heads_here * HEAD_SIZE
    kv_width = key_value_local * HEAD_SIZE
    segment, position, live_rows = group_layout(
        lengths, deal_order, lax.axis_index("dp"), group_rows
    )
    row_index = jnp.arange(group_rows, dtype=jnp.int32)
    allowed = (segment[:, None] == segment[None, :]) & (row_index[None, :] <= row_index[:, None])
    own_live = lax.dynamic_slice_in_dim(
        live_rows, lax.axis_index("tensor") * local_rows, local_rows
    ).astype(jnp.float32)[:, None]
    cosine_table, sine_table = rope_tables(position)
    cosine_table = cosine_table[:, None, :]
    sine_table = sine_table[:, None, :]
    full_set = (
        lax.all_gather(norm_attn, "dp", axis=0, tiled=True),
        lax.all_gather(w_query, "dp", axis=0, tiled=True),
        lax.all_gather(key_matrix, "dp", axis=0, tiled=True),
        lax.all_gather(value_matrix, "dp", axis=0, tiled=True),
        lax.all_gather(gain_query, "dp", axis=0, tiled=True),
        lax.all_gather(gain_key, "dp", axis=0, tiled=True),
        lax.all_gather(w_output, "dp", axis=1, tiled=True),
        lax.all_gather(norm_ffn, "dp", axis=0, tiled=True),
        lax.all_gather(w_gate, "dp", axis=0, tiled=True),
        lax.all_gather(w_up, "dp", axis=0, tiled=True),
        lax.all_gather(w_down, "dp", axis=1, tiled=True),
    )
    qkv_weight = jnp.concatenate((full_set[1], full_set[2], full_set[3]), axis=1)
    token_rows = tokens.astype(jnp.float32)
    scale_attn = rms_scale(token_rows)
    attention_normed_input = (token_rows * scale_attn * full_set[0].astype(jnp.float32)).astype(
        jnp.bfloat16
    )
    normed_attn_all = lax.all_gather(attention_normed_input, "tensor", axis=0, tiled=True)
    projected = jnp.dot(normed_attn_all, qkv_weight, preferred_element_type=jnp.float32)
    q_pre = projected[:, :q_width].reshape(group_rows, heads_here, HEAD_SIZE)
    key_before_norm = projected[:, q_width : q_width + kv_width].reshape(
        group_rows, key_value_local, HEAD_SIZE
    )
    value_rows = projected[:, q_width + kv_width :].astype(jnp.bfloat16)
    q_scale = rms_scale(q_pre)
    q_unit = q_pre * q_scale * full_set[4].astype(jnp.float32)
    queries = (q_unit * cosine_table + rotate_half(q_unit) * sine_table).astype(jnp.bfloat16)
    k_scale = rms_scale(key_before_norm)
    k_unit = key_before_norm * k_scale * full_set[5].astype(jnp.float32)
    key_rot = (k_unit * cosine_table + rotate_half(k_unit) * sine_table).astype(jnp.bfloat16)
    query_heads = jnp.moveaxis(
        queries.reshape(group_rows, key_value_local, rows_per_group, HEAD_SIZE), 1, 0
    )
    key_heads = jnp.moveaxis(key_rot, 1, 0)
    value_heads = jnp.moveaxis(value_rows.reshape(group_rows, key_value_local, HEAD_SIZE), 1, 0)
    context_heads, log_total = lax.map(
        lambda head_parts: attend_head(head_parts[0], head_parts[1], head_parts[2], allowed),
        (query_heads, key_heads, value_heads),
    )
    context = jnp.moveaxis(context_heads, 0, 1).reshape(group_rows, q_width)
    hidden = token_rows + lax.psum_scatter(
        jnp.dot(context, full_set[6], preferred_element_type=jnp.float32).astype(jnp.bfloat16),
        "tensor",
        scatter_dimension=0,
        tiled=True,
    ).astype(jnp.float32)
    scale_ffn = rms_scale(hidden)
    normed_ffn = (hidden * scale_ffn * full_set[7].astype(jnp.float32)).astype(jnp.bfloat16)
    normed_ffn_all = lax.all_gather(normed_ffn, "tensor", axis=0, tiled=True)
    gate_proj = jnp.dot(normed_ffn_all, full_set[8], preferred_element_type=jnp.float32)
    up_proj = jnp.dot(normed_ffn_all, full_set[9], preferred_element_type=jnp.float32)
    gate_sig = jax.nn.sigmoid(gate_proj)
    activation = (gate_proj * gate_sig * up_proj).astype(jnp.bfloat16)
    block_rows = hidden + lax.psum_scatter(
        jnp.dot(activation, full_set[10], preferred_element_type=jnp.float32).astype(jnp.bfloat16),
        "tensor",
        scatter_dimension=0,
        tiled=True,
    ).astype(jnp.float32)
    block_out = (block_rows * own_live).astype(jnp.bfloat16)
    back_set = (
        lax.all_gather(norm_attn, "dp", axis=0, tiled=True),
        lax.all_gather(w_query, "dp", axis=0, tiled=True),
        lax.all_gather(key_matrix, "dp", axis=0, tiled=True),
        lax.all_gather(value_matrix, "dp", axis=0, tiled=True),
        lax.all_gather(gain_query, "dp", axis=0, tiled=True),
        lax.all_gather(gain_key, "dp", axis=0, tiled=True),
        lax.all_gather(w_output, "dp", axis=1, tiled=True),
        lax.all_gather(norm_ffn, "dp", axis=0, tiled=True),
        lax.all_gather(w_gate, "dp", axis=0, tiled=True),
        lax.all_gather(w_up, "dp", axis=0, tiled=True),
        lax.all_gather(w_down, "dp", axis=1, tiled=True),
    )
    back_qkv = jnp.concatenate((back_set[1], back_set[2], back_set[3]), axis=1)
    d_rows = cotangent.astype(jnp.float32) * own_live
    d_branch = d_rows.astype(jnp.bfloat16)
    d_branch_all = lax.all_gather(d_branch, "tensor", axis=0, tiled=True)
    d_act = times_transpose(d_branch_all, back_set[10])
    grad_down = contract_rows(activation, d_branch_all)
    d_gate = (d_act * up_proj * gate_sig * (1.0 + gate_proj * (1.0 - gate_sig))).astype(
        jnp.bfloat16
    )
    d_up = (d_act * gate_proj * gate_sig).astype(jnp.bfloat16)
    grad_gate = contract_rows(normed_ffn_all, d_gate)
    grad_up = contract_rows(normed_ffn_all, d_up)
    d_normed_ffn = lax.psum_scatter(
        (times_transpose(d_gate, back_set[8]) + times_transpose(d_up, back_set[9])).astype(
            jnp.bfloat16
        ),
        "tensor",
        scatter_dimension=0,
        tiled=True,
    ).astype(jnp.float32)
    part_norm_ffn = jnp.sum(d_normed_ffn * hidden * scale_ffn, axis=0)
    d_hidden = d_rows + norm_back(d_normed_ffn, hidden, scale_ffn, back_set[7].astype(jnp.float32))
    d_attended = d_hidden.astype(jnp.bfloat16)
    d_attended_all = lax.all_gather(d_attended, "tensor", axis=0, tiled=True)
    d_context = times_transpose(d_attended_all, back_set[6]).astype(jnp.bfloat16)
    grad_output = contract_rows(context, d_attended_all)
    d_context_heads = jnp.moveaxis(
        d_context.reshape(group_rows, key_value_local, rows_per_group, HEAD_SIZE), 1, 0
    )
    d_query_heads, d_key_heads, d_value_heads = lax.map(
        lambda head_parts: attend_back(
            head_parts[0], head_parts[1], head_parts[2], head_parts[3], head_parts[4], allowed
        ),
        (query_heads, key_heads, value_heads, d_context_heads, log_total),
    )
    d_queries = jnp.moveaxis(d_query_heads, 0, 1).reshape(group_rows, heads_here, HEAD_SIZE)
    d_keys = jnp.moveaxis(d_key_heads, 0, 1)
    d_value = jnp.moveaxis(d_value_heads, 0, 1).reshape(group_rows, kv_width)
    du_query = d_queries * cosine_table + rotate_back(d_queries * sine_table)
    part_gain_query = jnp.sum(du_query * q_pre * q_scale, axis=(0, 1))
    d_q_pre = norm_back(du_query, q_pre, q_scale, back_set[4].astype(jnp.float32))
    du_key = d_keys * cosine_table + rotate_back(d_keys * sine_table)
    part_gain_key = jnp.sum(du_key * key_before_norm * k_scale, axis=(0, 1))
    d_k_pre = norm_back(du_key, key_before_norm, k_scale, back_set[5].astype(jnp.float32))
    d_projected = jnp.concatenate(
        (d_q_pre.reshape(group_rows, q_width), d_k_pre.reshape(group_rows, kv_width), d_value),
        axis=1,
    ).astype(jnp.bfloat16)
    grad_qkv = contract_rows(normed_attn_all, d_projected)
    grad_query = grad_qkv[:, :q_width]
    grad_key = grad_qkv[:, q_width : q_width + kv_width]
    grad_value = grad_qkv[:, q_width + kv_width :]
    d_normed_attn = lax.psum_scatter(
        times_transpose(d_projected, back_qkv).astype(jnp.bfloat16),
        "tensor",
        scatter_dimension=0,
        tiled=True,
    ).astype(jnp.float32)
    part_norm_attn = jnp.sum(d_normed_attn * token_rows * scale_attn, axis=0)
    d_tokens = d_hidden + norm_back(
        d_normed_attn, token_rows, scale_attn, back_set[0].astype(jnp.float32)
    )
    gain_parts = lax.psum((part_norm_attn, part_norm_ffn, part_gain_query, part_gain_key), "tensor")
    shards = tuple(
        (
            lax.psum_scatter(
                gain_parts[0].astype(jnp.bfloat16), "dp", scatter_dimension=0, tiled=True
            ).astype(jnp.float32),
            lax.psum_scatter(
                grad_query.astype(jnp.bfloat16), "dp", scatter_dimension=0, tiled=True
            ).astype(jnp.float32),
            lax.psum_scatter(
                grad_key.astype(jnp.bfloat16), "dp", scatter_dimension=0, tiled=True
            ).astype(jnp.float32),
            lax.psum_scatter(
                grad_value.astype(jnp.bfloat16), "dp", scatter_dimension=0, tiled=True
            ).astype(jnp.float32),
            lax.psum_scatter(
                gain_parts[2].astype(jnp.bfloat16), "dp", scatter_dimension=0, tiled=True
            ).astype(jnp.float32),
            lax.psum_scatter(
                gain_parts[3].astype(jnp.bfloat16), "dp", scatter_dimension=0, tiled=True
            ).astype(jnp.float32),
            lax.psum_scatter(
                grad_output.astype(jnp.bfloat16), "dp", scatter_dimension=1, tiled=True
            ).astype(jnp.float32),
            lax.psum_scatter(
                gain_parts[1].astype(jnp.bfloat16), "dp", scatter_dimension=0, tiled=True
            ).astype(jnp.float32),
            lax.psum_scatter(
                grad_gate.astype(jnp.bfloat16), "dp", scatter_dimension=0, tiled=True
            ).astype(jnp.float32),
            lax.psum_scatter(
                grad_up.astype(jnp.bfloat16), "dp", scatter_dimension=0, tiled=True
            ).astype(jnp.float32),
            lax.psum_scatter(
                grad_down.astype(jnp.bfloat16), "dp", scatter_dimension=1, tiled=True
            ).astype(jnp.float32),
        )
    )
    return (block_out, d_tokens.astype(jnp.bfloat16)) + shards


def solution(mesh):
    return jax.shard_map(
        local,
        mesh=mesh,
        in_specs=(
            P(("dp", "tensor"), None),
            P("dp"),
            P("dp", "tensor"),
            P("dp", "tensor"),
            P("dp", "tensor"),
            P("dp"),
            P("dp"),
            P("tensor", "dp"),
            P("dp"),
            P("dp", "tensor"),
            P("dp", "tensor"),
            P("tensor", "dp"),
            P(("dp", "tensor"), None),
            P(),
            P(),
        ),
        out_specs=(
            P(("dp", "tensor"), None),
            P(("dp", "tensor"), None),
            P("dp"),
            P("dp", "tensor"),
            P("dp", "tensor"),
            P("dp", "tensor"),
            P("dp"),
            P("dp"),
            P("tensor", "dp"),
            P("dp"),
            P("dp", "tensor"),
            P("dp", "tensor"),
            P("tensor", "dp"),
        ),
        check_vma=False,
    )
```

profile of v0, /device:TPU:0, one launch (start us, length us, event | category | flops | bytes accessed | tf_op | source)
XLA Modules:
  0.0 1377.7 jit_solution(12239359164739884811)
XLA Ops:
  10.2 10.3 all-gather
  31.5 13.4 all-reduce.8
  48.0 3.2 constant_dynamic-update-slice_fusion.2
  51.2 14.9 %all-gather.18.cloned.1.call-done = bf16[2048,256]{1,0:T(8,128)(2,1)} async-done(((bf16[256,256]{1,0:T(8,128)(2,1)}), bf16[2048,256]{1,0:T(8,128)(2,1)}) %all-gather.18.cloned.1.call-update) | async-done | bytes 1048592 | tf_op jit(solution)/shard_map/all_gather | solution.py:140
  68.4 23.1 %all-gather.20.cloned.1.call-done = bf16[2048,256]{1,0:T(8,128)(2,1)} async-done(((bf16[256,256]{1,0:T(8,128)(2,1)}), bf16[2048,256]{1,0:T(8,128)(2,1)}) %all-gather.20.cloned.1.call-update) | async-done | bytes 1048592 | tf_op jit(solution)/shard_map/all_gather | solution.py:141
  93.9 80.5 %all-gather.14.cloned.1.call-done = bf16[1024,2048]{1,0:T(8,128)(2,1)} async-done(((bf16[256,2048]{1,0:T(8,128)(2,1)}), bf16[1024,2048]{1,0:T(8,128)(2,1)}) %all-gather.14.cloned.1.call-update) | async-done | bytes 4194320 | tf_op jit(solution)/shard_map/all_gather | solution.py:156
  174.3 7.6 fusion.112
  191.8 3.4 copy.69
  195.2 3.2 copy.68
  206.1 16.8 %while.28 = (s32[]{:T(128)}, bf16[2,1024,2,128]{1,3,2,0:T(8,128)(2,1)}, f32[2,2,1024]{2,1,0:T(2,128)S(1)}, bf16[2,1024,128]{1,2,0:T(8,128)(2,1)S(1)}, bf16[2,102...) while((s32[]{:T(128)}, ...), condition=%wide.region_8.9_spmd.clone, body=%wide.region_5.8_spmd.clone.sunk | while | flops 1102313472 | bytes 31004760 | solution.py:174
  211.1 3.7 fusion.170
  219.3 3.7 fusion.170
  224.0 6.3 convolution_convert_fusion.4
  231.1 8.9 all-gather.1
  240.0 65.8 %reduce-scatter.12.cloned.1.call-done = bf16[256,2048]{1,0:T(8,128)(2,1)} async-done(((bf16[1024,2048]{1,0:T(8,128)(2,1)}), bf16[256,2048]{1,0:T(8,128)(2,1)}) %reduce-scatter.12.cloned.1.call-update) | async-done | bytes 1048592 | tf_op jit(solution)/shard_map/reduce_scatter | solution.py:179
  313.6 40.3 %all-gather.26.cloned.1.call-done = bf16[2048,1536]{1,0:T(8,128)(2,1)} async-done(((bf16[256,1536]{1,0:T(8,128)(2,1)}), bf16[2048,1536]{1,0:T(8,128)(2,1)}) %all-gather.26.cloned.1.call-update) | async-done | bytes 6291472 | tf_op jit(solution)/shard_map/all_gather | solution.py:146
  353.9 83.0 %all-gather.24.cloned.1.call-done = bf16[1024,2048]{1,0:T(8,128)(2,1)} async-done(((bf16[256,2048]{1,0:T(8,128)(2,1)}), bf16[1024,2048]{1,0:T(8,128)(2,1)}) %all-gather.24.cloned.1.call-update) | async-done | bytes 4194320 | tf_op jit(solution)/shard_map/all_gather | solution.py:187
  436.9 11.9 fusion.113
  448.8 34.2 %all-gather.28.cloned.1.call-done = bf16[2048,1536]{1,0:T(8,128)(2,1)} async-done(((bf16[256,1536]{1,0:T(8,128)(2,1)}), bf16[2048,1536]{1,0:T(8,128)(2,1)}) %all-gather.28.cloned.1.call-update) | async-done | bytes 6291472 | tf_op jit(solution)/shard_map/all_gather | solution.py:147
  483.0 11.7 fusion.114
  494.7 71.2 %all-gather.32.cloned.1.call-done = bf16[1024,2048]{1,0:T(8,128)(2,1)} async-done(((bf16[256,2048]{1,0:T(8,128)(2,1)}), bf16[1024,2048]{1,0:T(8,128)(2,1)}) %all-gather.32.cloned.1.call-update) | async-done | bytes 4194320 | tf_op jit(solution)/shard_map/all_gather | solution.py:215
  565.9 47.3 %all-gather.30.cloned.1.call-done = bf16[1536,2048]{1,0:T(8,128)(2,1)} async-done(((bf16[1536,256]{1,0:T(8,128)(2,1)}), bf16[1536,2048]{1,0:T(8,128)(2,1)}) %all-gather.30.cloned.1.call-update) | async-done | bytes 6291472 | tf_op jit(solution)/shard_map/all_gather | solution.py:148
  613.2 16.5 %multiply_convert_fusion = (bf16[1024,1536]{1,0:T(8,128)(2,1)}, bf16[1024,1536]{1,0:T(8,128)(2,1)S(1)}, bf16[1024,1536]{1,0:T(8,128)(2,1)}) fusion(f32[1024,1536]{1,0:T(8,128)} %fusion.113, f32[1024,1536]{1,0:T(8,128)} %fusion.114, bf16[1024,2048]{1,0:T(8,128)(2,1)} %all-gather.32.cloned.1.call-done, bf16[1536,2048]{1,0:T(8,128)(2,1)} %all-gather.30.cloned.1.call-done), kind=kOutput, calls=%fused_computation.75 | convolution fusion | flops 6467616768 | bytes 32505856 | tf_op jit(solution)/shard_map/dot_general | solution.py:52
  629.7 10.0 fusion.115
  639.7 10.5 add_convert_fusion
  650.2 11.1 convolution_convert_fusion.3
  661.4 65.7 %reduce-scatter.16.cloned.1.call-done = bf16[256,2048]{1,0:T(8,128)(2,1)} async-done(((bf16[1024,2048]{1,0:T(8,128)(2,1)}), bf16[256,2048]{1,0:T(8,128)(2,1)}) %reduce-scatter.16.cloned.1.call-update) | async-done | bytes 1048592 | tf_op jit(solution)/shard_map/reduce_scatter | solution.py:224
  729.6 77.1 %reduce-scatter.14.cloned.1.call-done = bf16[256,2048]{1,0:T(8,128)(2,1)} async-done(((bf16[1024,2048]{1,0:T(8,128)(2,1)}), bf16[256,2048]{1,0:T(8,128)(2,1)}) %reduce-scatter.14.cloned.1.call-update) | async-done | bytes 1048592 | tf_op jit(solution)/shard_map/reduce_scatter | solution.py:192
  806.7 5.0 fusion.106
  811.8 11.5 convolution_convert_fusion.2
  823.3 11.9 convolution_convert_fusion.1
  838.6 11.3 convolution_convert_fusion
  850.0 43.1 %all-gather.34.cloned.1.call-done = bf16[1024,2048]{1,0:T(8,128)(2,1)} async-done(((bf16[256,2048]{1,0:T(8,128)(2,1)}), bf16[1024,2048]{1,0:T(8,128)(2,1)}) %all-gather.34.cloned.1.call-update) | async-done | bytes 4194320 | tf_op jit(solution)/shard_map/all_gather | solution.py:235
  893.2 6.2 convolution_convert_fusion.8
  901.8 27.5 %while.29 = (s32[]{:T(128)}, f32[2,1024,2,128]{1,3,2,0:T(8,128)}, f32[2,1024,128]{2,1,0:T(8,128)}, bf16[2,1024,128]{2,1,0:T(8,128)(2,1)}, bf16[2,1024,128]{2,1,0...) while((s32[]{:T(128)}, f32[2,1024,2,128]{1,3,2,0:T(8,128)}, ...), condition=%wide.region_16.17_spmd.clone, body=%wide.region_14.16_spmd.clone.sunk | while | flops 2719348736 | bytes 101516552 | solution.py:241
  942.2 6.3 convolution_convert_fusion.5
  952.9 6.2 convolution_convert_fusion.7
  959.2 3.1 slice.71
  962.4 8.4 convolution_convert_fusion.6
  974.8 47.3 %reduce-scatter.30.cloned.1.call-done = bf16[256,1536]{1,0:T(8,128)(2,1)} async-done(((bf16[2048,1536]{1,0:T(8,128)(2,1)}), bf16[256,1536]{1,0:T(8,128)(2,1)}) %reduce-scatter.30.cloned.1.call-update) | async-done | bytes 786448 | tf_op jit(solution)/shard_map/reduce_scatter | solution.py:304
  1024.6 62.9 %reduce-scatter.32.cloned.1.call-done = bf16[1536,256]{1,0:T(8,128)(2,1)} async-done(((bf16[1536,2048]{1,0:T(8,128)(2,1)}), bf16[1536,256]{1,0:T(8,128)(2,1)}) %reduce-scatter.32.cloned.1.call-update) | async-done | bytes 786448 | tf_op jit(solution)/shard_map/reduce_scatter | solution.py:307
  1089.9 36.7 %reduce-scatter.22.cloned.1.call-done = bf16[256,256]{1,0:T(8,128)(2,1)} async-done(((bf16[2048,256]{1,0:T(8,128)(2,1)}), bf16[256,256]{1,0:T(8,128)(2,1)}) %reduce-scatter.22.cloned.1.call-update) | async-done | bytes 131088 | tf_op jit(solution)/shard_map/reduce_scatter | solution.py:283
  1128.2 37.6 %reduce-scatter.24.cloned.1.call-done = bf16[256,256]{1,0:T(8,128)(2,1)} async-done(((bf16[2048,256]{1,0:T(8,128)(2,1)}), bf16[256,256]{1,0:T(8,128)(2,1)}) %reduce-scatter.24.cloned.1.call-update) | async-done | bytes 131088 | tf_op jit(solution)/shard_map/reduce_scatter | solution.py:286
  1167.4 42.8 %reduce-scatter.26.cloned.1.call-done = bf16[512,256]{1,0:T(8,128)(2,1)} async-done(((bf16[512,2048]{1,0:T(8,128)(2,1)}), bf16[512,256]{1,0:T(8,128)(2,1)}) %reduce-scatter.26.cloned.1.call-update) | async-done | bytes 262160 | tf_op jit(solution)/shard_map/reduce_scatter | solution.py:295
  1211.9 43.1 %reduce-scatter.20.cloned.1.call-done = bf16[256,512]{1,0:T(8,128)(2,1)} async-done(((bf16[2048,512]{1,0:T(8,128)(2,1)}), bf16[256,512]{1,0:T(8,128)(2,1)}) %reduce-scatter.20.cloned.1.call-update) | async-done | bytes 262160 | tf_op jit(solution)/shard_map/reduce_scatter | solution.py:280
  1256.9 77.3 %reduce-scatter.18.cloned.1.call-done = bf16[256,2048]{1,0:T(8,128)(2,1)} async-done(((bf16[1024,2048]{1,0:T(8,128)(2,1)}), bf16[256,2048]{1,0:T(8,128)(2,1)}) %reduce-scatter.18.cloned.1.call-update) | async-done | bytes 1048592 | tf_op jit(solution)/shard_map/reduce_scatter | solution.py:264
  1336.0 18.2 %all-reduce.6 = (bf16[2048]{0:T(1024)(128)(2,1)S(1)}, bf16[128]{0:T(256)(128)(2,1)S(1)}, bf16[128]{0:T(256)(128)(2,1)S(1)}, bf16[2048]{0:T(1024)(128)(2,1)S(1)}) all-reduce(f32[2048]{0:T(1024)S(1)} %get-tuple-element.175, f32[128]{0:T(128)S(1)} %bitcast_reduce_fusion, ...), channel_id=1, replica_groups=mesh['dp'=8,'tensor'=4] {'tensor'}, use_global_device_ids=true, to_apply=%region_22.23 | all-reduce | flops 4352 | bytes 26112 | tf_op jit(solution)/shard_map/psum | solution.py:274
  1354.2 12.3 all-reduce.7
  (279 shorter events, 130.3 us)
Async XLA Ops:
  7.2 22.6 %copy-start.48 = (u32[32]{0:T(128)S(1)}, u32[32]{0:T(128)}, u32[]{:S(2)}) copy-start(u32[32]{0:T(128)} %constant.97) | copy-start | bytes 388
  7.2 19.2 %copy-start.51 = (s32[8]{0:T(128)S(1)}, s32[8]{0:T(128)}, u32[]{:S(2)}) copy-start(s32[8]{0:T(128)} %param.33) | copy-start | bytes 100
  7.2 19.8 %copy-start.52 = (s32[8]{0:T(128)S(1)}, s32[8]{0:T(128)}, u32[]{:S(2)}) copy-start(s32[8]{0:T(128)} %param.32) | copy-start | bytes 100
  7.2 23.8 %copy-start.53 = (bf16[16]{0:T(256)(128)(2,1)S(1)}, bf16[16]{0:T(256)(128)(2,1)}, u32[]{:S(2)}) copy-start(bf16[16]{0:T(256)(128)(2,1)} %param.25) | copy-start | bytes 100
  7.2 24.1 %copy-start.54 = (bf16[16]{0:T(256)(128)(2,1)S(1)}, bf16[16]{0:T(256)(128)(2,1)}, u32[]{:S(2)}) copy-start(bf16[16]{0:T(256)(128)(2,1)} %param.24) | copy-start | bytes 100
  7.2 40.8 %all-gather.16.cloned.1.call-start = ((), (), s32[]{:S(2)}) async-start(), calls=%async_computation.12 | async-start | bytes 2359296 | tf_op jit(solution)/shard_map/all_gather | solution.py:139
  8.0 58.1 %all-gather.18.cloned.1.call-start = ((), (), s32[]{:S(2)}) async-start(), calls=%async_computation.13 | async-start | bytes 1179648 | tf_op jit(solution)/shard_map/all_gather | solution.py:140
  8.7 82.8 %all-gather.20.cloned.1.call-start = ((), (), s32[]{:S(2)}) async-start(), calls=%async_computation.14 | async-start | bytes 1179648 | tf_op jit(solution)/shard_map/all_gather | solution.py:141
  9.5 164.9 %all-gather.14.cloned.1.call-start = ((), (), s32[]{:S(2)}) async-start(), calls=%async_computation.11 | async-start | bytes 5242880 | tf_op jit(solution)/shard_map/all_gather | solution.py:156
  25.7 197.3 %all-gather.22.cloned.1.call-start = ((), (), s32[]{:S(2)}) async-start(), calls=%async_computation.15 | async-start | bytes 2359296 | tf_op jit(solution)/shard_map/all_gather | solution.py:144
  26.3 279.5 %reduce-scatter.12.cloned.1.call-start = ((), (), s32[]{:S(2)}) async-start(), calls=%async_computation.16 | async-start | bytes 5242880 | tf_op jit(solution)/shard_map/reduce_scatter | solution.py:179
  44.9 155.3 %copy-start.45 = (f32[128]{0:T(128)}, f32[128]{0:T(128)S(1)}, u32[]{:S(2)}) copy-start(f32[128]{0:T(128)S(1)} %convert_element_type.188) | copy-start | bytes 1540
  48.0 155.0 %copy-start.43 = (f32[128]{0:T(128)}, f32[128]{0:T(128)S(1)}, u32[]{:S(2)}) copy-start(f32[128]{0:T(128)S(1)} %convert_element_type.191) | copy-start | bytes 1540
  185.4 14.9 %copy-start.34 = (f32[1024,2]{0,1:T(2,128)}, f32[1024,2]{0,1:T(2,128)S(1)}, u32[]{:S(2)}) copy-start(f32[1024,2]{0,1:T(2,128)S(1)} %get-tuple-element.251) | copy-start | bytes 24580
  185.7 14.5 %copy-start.4 = (f32[1024,2,128]{2,0,1:T(8,128)}, f32[1024,2,128]{2,0,1:T(8,128)S(1)}, u32[]{:S(2)}) copy-start(f32[1024,2,128]{2,0,1:T(8,128)S(1)} %copy.66) | copy-start | bytes 3145732
  191.8 6.5 slice-start
  230.3 75.5 %copy-start = (bf16[256,2048]{1,0:T(8,128)(2,1)S(1)}, bf16[256,2048]{1,0:T(8,128)(2,1)}, u32[]{:S(2)}) copy-start(bf16[256,2048]{1,0:T(8,128)(2,1)} %param.19) | copy-start | bytes 3145732
  230.3 81.3 %copy-start.23 = (bf16[256,2048]{1,0:T(8,128)(2,1)S(1)}, bf16[256,2048]{1,0:T(8,128)(2,1)}, u32[]{:S(2)}) copy-start(bf16[256,2048]{1,0:T(8,128)(2,1)} %param.31) | copy-start | bytes 3145732
  230.3 123.6 %all-gather.26.cloned.1.call-start = ((), (), s32[]{:S(2)}) async-start(), calls=%async_computation.18 | async-start | bytes 7077888 | tf_op jit(solution)/shard_map/all_gather | solution.py:146
  231.0 205.9 %all-gather.24.cloned.1.call-start = ((), (), s32[]{:S(2)}) async-start(), calls=%async_computation.17 | async-start | bytes 5242880 | tf_op jit(solution)/shard_map/all_gather | solution.py:187
  310.0 173.0 %all-gather.28.cloned.1.call-start = ((), (), s32[]{:S(2)}) async-start(), calls=%async_computation.19 | async-start | bytes 7077888 | tf_op jit(solution)/shard_map/all_gather | solution.py:147
  310.8 255.1 %all-gather.32.cloned.1.call-start = ((), (), s32[]{:S(2)}) async-start(), calls=%async_computation.22 | async-start | bytes 5242880 | tf_op jit(solution)/shard_map/all_gather | solution.py:215
  312.8 300.3 %all-gather.30.cloned.1.call-start = ((), (), s32[]{:S(2)}) async-start(), calls=%async_computation.20 | async-start | bytes 7077888 | tf_op jit(solution)/shard_map/all_gather | solution.py:148
  313.6 413.5 %reduce-scatter.16.cloned.1.call-start = ((), (), s32[]{:S(2)}) async-start(), calls=%async_computation.23 | async-start | bytes 5242880 | tf_op jit(solution)/shard_map/reduce_scatter | solution.py:224
  629.6 10.0 copy-start.56
  629.7 10.0 copy-start.49
  650.2 156.5 %reduce-scatter.14.cloned.1.call-start = ((), (), s32[]{:S(2)}) async-start(), calls=%async_computation.21 | async-start | bytes 5242880 | tf_op jit(solution)/shard_map/reduce_scatter | solution.py:192
  661.3 65.8 %copy-start.9 = (bf16[256,2048]{1,0:T(8,128)(2,1)S(1)}, bf16[256,2048]{1,0:T(8,128)(2,1)}, u32[]{:S(2)}) copy-start(bf16[256,2048]{1,0:T(8,128)(2,1)} %reduce-scatter.12.cloned.1.call-done) | copy-start | bytes 3145732
  661.3 231.8 %all-gather.34.cloned.1.call-start = ((), (), s32[]{:S(2)}) async-start(), calls=%async_computation.24 | async-start | bytes 5242880 | tf_op jit(solution)/shard_map/all_gather | solution.py:235
  811.8 160.4 %reduce-scatter.28.cloned.1.call-start = ((), (), s32[]{:S(2)}) async-start(), calls=%async_computation.30 | async-start | bytes 7077888 | tf_op jit(solution)/shard_map/reduce_scatter | solution.py:301
  823.3 198.8 %reduce-scatter.30.cloned.1.call-start = ((), (), s32[]{:S(2)}) async-start(), calls=%async_computation.31 | async-start | bytes 7077888 | tf_op jit(solution)/shard_map/reduce_scatter | solution.py:304
  835.3 252.2 %reduce-scatter.32.cloned.1.call-start = ((), (), s32[]{:S(2)}) async-start(), calls=%async_computation.32 | async-start | bytes 7077888 | tf_op jit(solution)/shard_map/reduce_scatter | solution.py:307
  850.0 51.9 %copy-start.15 = (bf16[2,1024,2,128]{3,1,2,0:T(8,128)(2,1)S(1)}, bf16[2,1024,2,128]{3,1,2,0:T(8,128)(2,1)}, u32[]{:S(2)}) copy-start(bf16[2,1024,2,128]{3,1,2,0:T(8,128)(2,1)} %copy-done.14) | copy-start | bytes 3145732
  850.0 276.6 %reduce-scatter.22.cloned.1.call-start = ((), (), s32[]{:S(2)}) async-start(), calls=%async_computation.27 | async-start | bytes 1179648 | tf_op jit(solution)/shard_map/reduce_scatter | solution.py:283
  931.2 5.2 copy-start.8
  931.2 5.2 copy-start.25
  952.1 213.6 %reduce-scatter.24.cloned.1.call-start = ((), (), s32[]{:S(2)}) async-start(), calls=%async_computation.28 | async-start | bytes 1179648 | tf_op jit(solution)/shard_map/reduce_scatter | solution.py:286
  952.9 257.2 %reduce-scatter.26.cloned.1.call-start = ((), (), s32[]{:S(2)}) async-start(), calls=%async_computation.29 | async-start | bytes 2359296 | tf_op jit(solution)/shard_map/reduce_scatter | solution.py:295
  959.1 3.3 copy-start.29
  959.1 3.3 copy-start.31
  959.1 295.9 %reduce-scatter.20.cloned.1.call-start = ((), (), s32[]{:S(2)}) async-start(), calls=%async_computation.26 | async-start | bytes 2359296 | tf_op jit(solution)/shard_map/reduce_scatter | solution.py:280
  962.3 371.8 %reduce-scatter.18.cloned.1.call-start = ((), (), s32[]{:S(2)}) async-start(), calls=%async_computation.25 | async-start | bytes 5242880 | tf_op jit(solution)/shard_map/reduce_scatter | solution.py:264
  972.1 362.0 %copy-start.1 = (bf16[256,2048]{1,0:T(8,128)(2,1)S(1)}, bf16[256,2048]{1,0:T(8,128)(2,1)}, u32[]{:S(2)}) copy-start(bf16[256,2048]{1,0:T(8,128)(2,1)} %param.19) | copy-start | bytes 3145732
  972.1 362.0 %copy-start.37 = (f32[8,1,256]{2,1,0:T(1,128)S(1)}, f32[8,1,256]{2,1,0:T(1,128)}, u32[]{:S(2)}) copy-start(f32[8,1,256]{2,1,0:T(1,128)} %copy-done.36) | copy-start | bytes 24580
  972.1 362.0 %copy-start.42 = (f32[256]{0:T(256)S(1)}, f32[256]{0:T(256)}, u32[]{:S(2)}) copy-start(f32[256]{0:T(256)} %copy-done.41) | copy-start | bytes 3076
  974.8 361.3 %copy-start.40 = (f32[2048]{0:T(1024)S(1)}, f32[2048]{0:T(1024)}, u32[]{:S(2)}) copy-start(f32[2048]{0:T(1024)} %get-tuple-element.171) | copy-start | bytes 24580
  974.8 393.0 %copy-start.17 = (f32[256,2048]{1,0:T(8,128)S(1)}, f32[256,2048]{1,0:T(8,128)}, u32[]{:S(2)}) copy-start(f32[256,2048]{1,0:T(8,128)} %get-tuple-element.223) | copy-start | bytes 6291460
  974.8 393.0 %copy-start.47 = (f32[256]{0:T(256)S(1)}, f32[256]{0:T(256)}, u32[]{:S(2)}) copy-start(f32[256]{0:T(256)} %get-tuple-element.252) | copy-start | bytes 3076
  (37 other events, 68.7 us)
Sparse Core Ops, SparseCore 0:
  10.0 30.6 all-gather.15
  42.5 23.5 all-gather.17
  68.0 23.4 all-gather.19
  93.5 80.7 all-gather.13
  176.0 26.7 all-gather.21
  230.4 75.3 reduce-scatter.11
  307.8 46.0 all-gather.25
  356.1 80.7 all-gather.23
  438.9 44.0 all-gather.27
  485.1 80.7 all-gather.31
  567.9 45.1 all-gather.29
  650.3 76.7 reduce-scatter.15
  729.4 77.2 reduce-scatter.13
  811.9 81.2 all-gather.33
  896.8 60.2 reduce-scatter.27
  960.3 61.7 reduce-scatter.29
  1025.7 61.7 reduce-scatter.31
  1090.5 36.0 reduce-scatter.21
  1129.7 35.9 reduce-scatter.23
  1168.9 41.2 reduce-scatter.25
  1213.8 41.2 reduce-scatter.19
  1257.4 76.7 reduce-scatter.17
where the time goes:
time: 1390 us; the launch traced here: 1380 us
  waiting for transfers between devices  999 us (72%)
  matrix products  176 us (13%)
  other arithmetic  76.1 us (5%)
  blocking collectives  63.1 us (5%)
  local copies, waits for them, and re-layouts  44.2 us (3%)
  between operations  17.3 us (1%)
    all_gather x1, waiting for transfers between devices, local(): normed_ffn_all = lax.all_gather(normed_ffn, 'tensor', axis=0, tiled=True)  83 us
    all_gather x1, waiting for transfers between devices, local(): lax.all_gather(attention_normed_input, 'tensor', axis=0, tiled=True)  80.5 us
    reduce_scatter x1, waiting for transfers between devices, local(): lax.psum_scatter(times_transpose(d_projected, back_qkv).astype(jnp.bfloat...  77.3 us
    reduce_scatter x1, waiting for transfers between devices, local(): lax.psum_scatter(jnp.dot(activation, full_set[10], preferred_element_type...  77.1 us
    all_gather x1, waiting for transfers between devices, local(): d_branch_all = lax.all_gather(d_branch, 'tensor', axis=0, tiled=True)  71.2 us
    reduce_scatter x1, waiting for transfers between devices, local(): lax.psum_scatter(jnp.dot(context, full_set[6], preferred_element_type=jnp...  65.8 us
    reduce_scatter x1, waiting for transfers between devices, local(): lax.psum_scatter((times_transpose(d_gate, back_set[8]) + times_transpose(...  65.7 us
    reduce_scatter x1, waiting for transfers between devices, local(): lax.psum_scatter(grad_down.astype(jnp.bfloat16), 'dp', scatter_dimension=...  62.9 us
  transfers between devices with their start and end apart: 22, of which 19 were waited for; matrix products, arithmetic and copies ran while one was open for 17% of the time, Pallas kernels for 0%

commit v1 on v0

--- a/solution.py
+++ b/solution.py
@@ -184,7 +184,24 @@
     ).astype(jnp.float32)
     scale_ffn = rms_scale(hidden)
     normed_ffn = (hidden * scale_ffn * full_set[7].astype(jnp.float32)).astype(jnp.bfloat16)
-    normed_ffn_all = lax.all_gather(normed_ffn, "tensor", axis=0, tiled=True)
+    ways, here, step = (lax.axis_size("tensor"), lax.axis_index("tensor"), normed_ffn.shape[0])
+    shape = [n * ways if d == 0 else n for d, n in enumerate(normed_ffn.shape)]
+    normed_ffn_all = lax.dynamic_update_slice_in_dim(
+        jnp.zeros(shape, normed_ffn.dtype), normed_ffn, here * step, axis=0
+    )
+    going_up = going_down = normed_ffn
+    for far in range(1, ways // 2 + 1):
+        going_up = lax.ppermute(going_up, "tensor", [(d, (d + 1) % ways) for d in range(ways)])
+        normed_ffn_all = lax.dynamic_update_slice_in_dim(
+            normed_ffn_all, going_up, (here - far) % ways * step, axis=0
+        )
+        if 2 * far < ways:
+            going_down = lax.ppermute(
+                going_down, "tensor", [(d, (d - 1) % ways) for d in range(ways)]
+            )
+            normed_ffn_all = lax.dynamic_update_slice_in_dim(
+                normed_ffn_all, going_down, (here + far) % ways * step, axis=0
+            )
     gate_proj = jnp.dot(normed_ffn_all, full_set[8], preferred_element_type=jnp.float32)
     up_proj = jnp.dot(normed_ffn_all, full_set[9], preferred_element_type=jnp.float32)
     gate_sig = jax.nn.sigmoid(gate_proj)

time: 1390 us -> 1370 us (0.986)
  waiting for transfers between devices: 999 us -> 923 us
  starting transfers between devices: 0.88 us -> 48 us
    all_gather x1 -> x0, waiting for transfers between devices: 83 us -> none  [local(): normed_ffn_all = lax.all_gather(normed_ffn, 'tensor', axis=0, tiled=True)]
    reduce_scatter x1, waiting for transfers between devices: 0.02 us -> 47.3 us  [local(): lax.psum_scatter(grad_gate.astype(jnp.bfloat16), 'dp', scatter_dimension=...]
    reduce_scatter x1, waiting for transfers between devices: 47.3 us -> 0.02 us  [local(): lax.psum_scatter(grad_up.astype(jnp.bfloat16), 'dp', scatter_dimension=0,...]
    ppermute x0 -> x3, starting transfers between devices: none -> 47.2 us  [the longest x2 44.8 us: local(): lax.ppermute(going_up, 'tensor', [(d, (d + 1) % ways) for d in range(ways)])]
    ppermute x0 -> x3, waiting for transfers between devices: none -> 43 us  [the longest x2 43 us: local(): lax.ppermute(going_up, 'tensor', [(d, (d + 1) % ways) for d in range(ways)])]
    all_gather x1, waiting for transfers between devices: 71.2 us -> 49.4 us  [local(): d_branch_all = lax.all_gather(d_branch, 'tensor', axis=0, tiled=True)]
  transfers between devices with their start and end apart: 22 -> 24, of which waited for: 19 -> 19; matrix products, arithmetic and copies ran while one was open for 17% -> 18% of each run, Pallas kernels for 0% -> 0%
where the time goes in v1:
time: 1370 us; the launch traced here: 1360 us
  waiting for transfers between devices  923 us (67%)
  matrix products  176 us (13%)
  other arithmetic  75.4 us (6%)
  blocking collectives  63.1 us (5%)
  local copies, waits for them, and re-layouts  53 us (4%)
  starting transfers between devices  48 us (4%)
  between operations  17.3 us (1%)
    all_gather x1, waiting for transfers between devices, local(): lax.all_gather(attention_normed_input, 'tensor', axis=0, tiled=True)  80.5 us
    reduce_scatter x1, waiting for transfers between devices, local(): lax.psum_scatter(times_transpose(d_projected, back_qkv).astype(jnp.bfloat...  77.3 us
    reduce_scatter x1, waiting for transfers between devices, local(): lax.psum_scatter(jnp.dot(activation, full_set[10], preferred_element_type...  76.9 us
    reduce_scatter x1, waiting for transfers between devices, local(): lax.psum_scatter((times_transpose(d_gate, back_set[8]) + times_transpose(...  65.7 us
    reduce_scatter x1, waiting for transfers between devices, local(): lax.psum_scatter(grad_down.astype(jnp.bfloat16), 'dp', scatter_dimension=...  62.9 us
    reduce_scatter x1, waiting for transfers between devices, local(): lax.psum_scatter(jnp.dot(context, full_set[6], preferred_element_type=jnp...  62 us
    all_gather x1, waiting for transfers between devices, local(): d_branch_all = lax.all_gather(d_branch, 'tensor', axis=0, tiled=True)  49.4 us
    dot_general x5, matrix products, contract_rows(): lax.dot_general(left, right, (((0,), (0,)), ((), ())), preferred_element_...  47.3 us
  transfers between devices with their start and end apart: 24, of which 19 were waited for; matrix products, arithmetic and copies ran while one was open for 18% of the time, Pallas kernels for 0%

profile of v1, /device:TPU:0, one launch (start us, length us, event | category | flops | bytes accessed | tf_op | source)
XLA Modules:
  0.0 1356.8 jit_solution(16355960102758444378)
XLA Ops:
  10.2 10.3 all-gather
  31.5 13.4 all-reduce.8
  48.0 3.1 constant_dynamic-update-slice_fusion.2
  51.1 15.1 %all-gather.17.cloned.1.call-done = bf16[2048,256]{1,0:T(8,128)(2,1)} async-done(((bf16[256,256]{1,0:T(8,128)(2,1)}), bf16[2048,256]{1,0:T(8,128)(2,1)}) %all-gather.17.cloned.1.call-update) | async-done | bytes 1048592 | tf_op jit(solution)/shard_map/all_gather | solution.py:140
  68.5 23.1 %all-gather.19.cloned.1.call-done = bf16[2048,256]{1,0:T(8,128)(2,1)} async-done(((bf16[256,256]{1,0:T(8,128)(2,1)}), bf16[2048,256]{1,0:T(8,128)(2,1)}) %all-gather.19.cloned.1.call-update) | async-done | bytes 1048592 | tf_op jit(solution)/shard_map/all_gather | solution.py:141
  93.9 80.5 %all-gather.13.cloned.1.call-done = bf16[1024,2048]{1,0:T(8,128)(2,1)} async-done(((bf16[256,2048]{1,0:T(8,128)(2,1)}), bf16[1024,2048]{1,0:T(8,128)(2,1)}) %all-gather.13.cloned.1.call-update) | async-done | bytes 4194320 | tf_op jit(solution)/shard_map/all_gather | solution.py:156
  174.3 7.6 fusion.112
  191.9 3.3 copy.69
  195.2 3.2 copy.68
  206.1 16.8 %while.28 = (s32[]{:T(128)}, bf16[2,1024,2,128]{1,3,2,0:T(8,128)(2,1)}, f32[2,2,1024]{2,1,0:T(2,128)S(1)}, bf16[2,1024,128]{1,2,0:T(8,128)(2,1)S(1)}, bf16[2,102...) while((s32[]{:T(128)}, ...), condition=%wide.region_8.9_spmd.clone, body=%wide.region_5.8_spmd.clone.sunk | while | flops 1102313472 | bytes 31004760 | solution.py:174
  211.0 3.7 fusion.170
  219.2 3.7 fusion.170
  222.9 6.7 convolution_convert_fusion.4
  234.2 8.9 all-gather.1
  243.1 62.0 %reduce-scatter.12.cloned.1.call-done = bf16[256,2048]{1,0:T(8,128)(2,1)} async-done(((bf16[1024,2048]{1,0:T(8,128)(2,1)}), bf16[256,2048]{1,0:T(8,128)(2,1)}) %reduce-scatter.12.cloned.1.call-update) | async-done | bytes 1048592 | tf_op jit(solution)/shard_map/reduce_scatter | solution.py:179
  315.3 43.0 %collective-permute-done = bf16[256,2048]{1,0:T(8,128)(2,1)} collective-permute-done((bf16[256,2048]{1,0:T(8,128)(2,1)}, bf16[256,2048]{1,0:T(8,128)(2,1)}, u32[]{:S(2)}, u32[]{:S(2)}) %collective-permute-start) | collective-permute-done | bytes 1048608 | tf_op jit(solution)/shard_map/ppermute | solution.py:194
  358.3 43.4 %collective-permute-start.2 = (bf16[256,2048]{1,0:T(8,128)(2,1)}, bf16[256,2048]{1,0:T(8,128)(2,1)}, u32[]{:S(2)}, u32[]{:S(2)}) collective-permute-start(bf16[256,2048]{1,0:T(8,128)(2,1)} %collective-permute-done), channel_id=1, source_target_pairs={{0,1},{1,2},{2,3},{3,0},{4,5},{5,6},{6,7},{7,4},{8,9},{9,10},{10,1... | collective-permute-start | bytes 3145736 | tf_op jit(solution)/shard_map/ppermute | solution.py:194
  401.7 49.4 %all-gather.29.cloned.1.call-done = bf16[1024,2048]{1,0:T(8,128)(2,1)} async-done(((bf16[256,2048]{1,0:T(8,128)(2,1)}), bf16[1024,2048]{1,0:T(8,128)(2,1)}) %all-gather.29.cloned.1.call-update) | async-done | bytes 4194320 | tf_op jit(solution)/shard_map/all_gather | solution.py:232
  451.0 47.0 %all-gather.27.cloned.1.call-done = bf16[1536,2048]{1,0:T(8,128)(2,1)} async-done(((bf16[1536,256]{1,0:T(8,128)(2,1)}), bf16[1536,2048]{1,0:T(8,128)(2,1)}) %all-gather.27.cloned.1.call-update) | async-done | bytes 6291472 | tf_op jit(solution)/shard_map/all_gather | solution.py:148
  498.0 12.0 fusion.114
  517.0 28.7 %all-gather.25.cloned.1.call-done = bf16[2048,1536]{1,0:T(8,128)(2,1)} async-done(((bf16[256,1536]{1,0:T(8,128)(2,1)}), bf16[2048,1536]{1,0:T(8,128)(2,1)}) %all-gather.25.cloned.1.call-update) | async-done | bytes 6291472 | tf_op jit(solution)/shard_map/all_gather | solution.py:147
  545.6 11.8 fusion.113
  557.5 35.6 %all-gather.23.cloned.1.call-done = bf16[2048,1536]{1,0:T(8,128)(2,1)} async-done(((bf16[256,1536]{1,0:T(8,128)(2,1)}), bf16[2048,1536]{1,0:T(8,128)(2,1)}) %all-gather.23.cloned.1.call-update) | async-done | bytes 6291472 | tf_op jit(solution)/shard_map/all_gather | solution.py:146
  593.1 16.3 %multiply_convert_fusion = (bf16[1024,1536]{1,0:T(8,128)(2,1)S(1)}, bf16[1024,1536]{1,0:T(8,128)(2,1)S(1)}, bf16[1024,1536]{1,0:T(8,128)(2,1)}) fusion(f32[1024,1536]{1,0:T(8,128)} %fusion.114, f32[1024,1536]{1,0:T(8,128)} %fusion.113, bf16[1024,2048]{1,0:T(8,128)(2,1)} %constant_dynamic-update-slice_fusion.3, ...), kind=kOutput, calls=%fused_computation.75 | convolution fusion | flops 6467616768 | bytes 32505856 | tf_op jit(solution)/shard_map/dot_general | solution.py:205
  609.4 8.9 fusion.115
  618.3 10.7 add_convert_fusion
  629.1 11.1 convolution_convert_fusion.3
  640.3 65.7 %reduce-scatter.16.cloned.1.call-done = bf16[256,2048]{1,0:T(8,128)(2,1)} async-done(((bf16[1024,2048]{1,0:T(8,128)(2,1)}), bf16[256,2048]{1,0:T(8,128)(2,1)}) %reduce-scatter.16.cloned.1.call-update) | async-done | bytes 1048592 | tf_op jit(solution)/shard_map/reduce_scatter | solution.py:241
  708.5 76.9 %reduce-scatter.14.cloned.1.call-done = bf16[256,2048]{1,0:T(8,128)(2,1)} async-done(((bf16[1024,2048]{1,0:T(8,128)(2,1)}), bf16[256,2048]{1,0:T(8,128)(2,1)}) %reduce-scatter.14.cloned.1.call-update) | async-done | bytes 1048592 | tf_op jit(solution)/shard_map/reduce_scatter | solution.py:209
  785.4 5.0 fusion.106
  790.5 11.5 convolution_convert_fusion.1
  802.1 11.9 convolution_convert_fusion.2
  817.3 11.3 convolution_convert_fusion
  828.8 43.1 %all-gather.31.cloned.1.call-done = bf16[1024,2048]{1,0:T(8,128)(2,1)} async-done(((bf16[256,2048]{1,0:T(8,128)(2,1)}), bf16[1024,2048]{1,0:T(8,128)(2,1)}) %all-gather.31.cloned.1.call-update) | async-done | bytes 4194320 | tf_op jit(solution)/shard_map/all_gather | solution.py:252
  871.9 6.2 convolution_convert_fusion.8
  880.5 27.4 %while.29 = (s32[]{:T(128)}, f32[2,1024,2,128]{1,3,2,0:T(8,128)}, f32[2,1024,128]{2,1,0:T(8,128)}, bf16[2,1024,128]{2,1,0:T(8,128)(2,1)}, bf16[2,1024,128]{2,1,0...) while((s32[]{:T(128)}, f32[2,1024,2,128]{1,3,2,0:T(8,128)}, ...), condition=%wide.region_16.17_spmd.clone, body=%wide.region_14.16_spmd.clone.sunk | while | flops 2719348736 | bytes 101516552 | solution.py:258
  920.9 6.3 convolution_convert_fusion.5
  931.5 6.3 convolution_convert_fusion.7
  941.0 8.4 convolution_convert_fusion.6
  953.5 47.3 %reduce-scatter.28.cloned.1.call-done = bf16[256,1536]{1,0:T(8,128)(2,1)} async-done(((bf16[2048,1536]{1,0:T(8,128)(2,1)}), bf16[256,1536]{1,0:T(8,128)(2,1)}) %reduce-scatter.28.cloned.1.call-update) | async-done | bytes 786448 | tf_op jit(solution)/shard_map/reduce_scatter | solution.py:318
  1003.3 62.9 %reduce-scatter.32.cloned.1.call-done = bf16[1536,256]{1,0:T(8,128)(2,1)} async-done(((bf16[1536,2048]{1,0:T(8,128)(2,1)}), bf16[1536,256]{1,0:T(8,128)(2,1)}) %reduce-scatter.32.cloned.1.call-update) | async-done | bytes 786448 | tf_op jit(solution)/shard_map/reduce_scatter | solution.py:324
  1068.6 36.7 %reduce-scatter.22.cloned.1.call-done = bf16[256,256]{1,0:T(8,128)(2,1)} async-done(((bf16[2048,256]{1,0:T(8,128)(2,1)}), bf16[256,256]{1,0:T(8,128)(2,1)}) %reduce-scatter.22.cloned.1.call-update) | async-done | bytes 131088 | tf_op jit(solution)/shard_map/reduce_scatter | solution.py:300
  1106.9 38.0 %reduce-scatter.24.cloned.1.call-done = bf16[256,256]{1,0:T(8,128)(2,1)} async-done(((bf16[2048,256]{1,0:T(8,128)(2,1)}), bf16[256,256]{1,0:T(8,128)(2,1)}) %reduce-scatter.24.cloned.1.call-update) | async-done | bytes 131088 | tf_op jit(solution)/shard_map/reduce_scatter | solution.py:303
  1146.6 42.9 %reduce-scatter.26.cloned.1.call-done = bf16[512,256]{1,0:T(8,128)(2,1)} async-done(((bf16[512,2048]{1,0:T(8,128)(2,1)}), bf16[512,256]{1,0:T(8,128)(2,1)}) %reduce-scatter.26.cloned.1.call-update) | async-done | bytes 262160 | tf_op jit(solution)/shard_map/reduce_scatter | solution.py:312
  1191.2 43.0 %reduce-scatter.20.cloned.1.call-done = bf16[256,512]{1,0:T(8,128)(2,1)} async-done(((bf16[2048,512]{1,0:T(8,128)(2,1)}), bf16[256,512]{1,0:T(8,128)(2,1)}) %reduce-scatter.20.cloned.1.call-update) | async-done | bytes 262160 | tf_op jit(solution)/shard_map/reduce_scatter | solution.py:297
  1236.0 77.3 %reduce-scatter.18.cloned.1.call-done = bf16[256,2048]{1,0:T(8,128)(2,1)} async-done(((bf16[1024,2048]{1,0:T(8,128)(2,1)}), bf16[256,2048]{1,0:T(8,128)(2,1)}) %reduce-scatter.18.cloned.1.call-update) | async-done | bytes 1048592 | tf_op jit(solution)/shard_map/reduce_scatter | solution.py:281
  1315.2 18.2 %all-reduce.6 = (bf16[2048]{0:T(1024)(128)(2,1)S(1)}, bf16[128]{0:T(256)(128)(2,1)S(1)}, bf16[128]{0:T(256)(128)(2,1)S(1)}, bf16[2048]{0:T(1024)(128)(2,1)S(1)}) all-reduce(f32[2048]{0:T(1024)S(1)} %get-tuple-element.175, f32[128]{0:T(128)S(1)} %bitcast_reduce_fusion, ...), channel_id=1, replica_groups=mesh['dp'=8,'tensor'=4] {'tensor'}, use_global_device_ids=true, to_apply=%region_22.23 | all-reduce | flops 4352 | bytes 26112 | tf_op jit(solution)/shard_map/psum | solution.py:291
  1333.4 12.3 all-reduce.7
  (290 shorter events, 145.0 us)
Async XLA Ops:
  7.2 22.5 %copy-start.48 = (u32[32]{0:T(128)S(1)}, u32[32]{0:T(128)}, u32[]{:S(2)}) copy-start(u32[32]{0:T(128)} %constant.125) | copy-start | bytes 388
  7.2 19.2 %copy-start.52 = (s32[8]{0:T(128)S(1)}, s32[8]{0:T(128)}, u32[]{:S(2)}) copy-start(s32[8]{0:T(128)} %param.33) | copy-start | bytes 100
  7.2 19.8 %copy-start.53 = (s32[8]{0:T(128)S(1)}, s32[8]{0:T(128)}, u32[]{:S(2)}) copy-start(s32[8]{0:T(128)} %param.32) | copy-start | bytes 100
  7.2 23.8 %copy-start.54 = (bf16[16]{0:T(256)(128)(2,1)S(1)}, bf16[16]{0:T(256)(128)(2,1)}, u32[]{:S(2)}) copy-start(bf16[16]{0:T(256)(128)(2,1)} %param.25) | copy-start | bytes 100
  7.2 24.0 %copy-start.55 = (bf16[16]{0:T(256)(128)(2,1)S(1)}, bf16[16]{0:T(256)(128)(2,1)}, u32[]{:S(2)}) copy-start(bf16[16]{0:T(256)(128)(2,1)} %param.24) | copy-start | bytes 100
  7.2 40.7 %all-gather.15.cloned.1.call-start = ((), (), s32[]{:S(2)}) async-start(), calls=%async_computation.12 | async-start | bytes 2359296 | tf_op jit(solution)/shard_map/all_gather | solution.py:139
  8.0 58.2 %all-gather.17.cloned.1.call-start = ((), (), s32[]{:S(2)}) async-start(), calls=%async_computation.13 | async-start | bytes 1179648 | tf_op jit(solution)/shard_map/all_gather | solution.py:140
  8.7 82.8 %all-gather.19.cloned.1.call-start = ((), (), s32[]{:S(2)}) async-start(), calls=%async_computation.14 | async-start | bytes 1179648 | tf_op jit(solution)/shard_map/all_gather | solution.py:141
  9.5 164.9 %all-gather.13.cloned.1.call-start = ((), (), s32[]{:S(2)}) async-start(), calls=%async_computation.11 | async-start | bytes 5242880 | tf_op jit(solution)/shard_map/all_gather | solution.py:156
  25.7 197.2 %all-gather.21.cloned.1.call-start = ((), (), s32[]{:S(2)}) async-start(), calls=%async_computation.15 | async-start | bytes 2359296 | tf_op jit(solution)/shard_map/all_gather | solution.py:144
  26.3 278.9 %reduce-scatter.12.cloned.1.call-start = ((), (), s32[]{:S(2)}) async-start(), calls=%async_computation.16 | async-start | bytes 5242880 | tf_op jit(solution)/shard_map/reduce_scatter | solution.py:179
  44.9 155.3 %copy-start.45 = (f32[128]{0:T(128)}, f32[128]{0:T(128)S(1)}, u32[]{:S(2)}) copy-start(f32[128]{0:T(128)S(1)} %convert_element_type.188) | copy-start | bytes 1540
  48.0 155.0 %copy-start.43 = (f32[128]{0:T(128)}, f32[128]{0:T(128)S(1)}, u32[]{:S(2)}) copy-start(f32[128]{0:T(128)S(1)} %convert_element_type.191) | copy-start | bytes 1540
  185.4 14.8 %copy-start.34 = (f32[1024,2]{0,1:T(2,128)}, f32[1024,2]{0,1:T(2,128)S(1)}, u32[]{:S(2)}) copy-start(f32[1024,2]{0,1:T(2,128)S(1)} %get-tuple-element.253) | copy-start | bytes 24580
  185.7 14.5 %copy-start.4 = (f32[1024,2,128]{2,0,1:T(8,128)}, f32[1024,2,128]{2,0,1:T(8,128)S(1)}, u32[]{:S(2)}) copy-start(f32[1024,2,128]{2,0,1:T(8,128)S(1)} %copy.66) | copy-start | bytes 3145732
  191.9 6.5 slice-start
  222.9 6.7 copy-start.14
  229.6 75.6 %copy-start = (bf16[256,2048]{1,0:T(8,128)(2,1)S(1)}, bf16[256,2048]{1,0:T(8,128)(2,1)}, u32[]{:S(2)}) copy-start(bf16[256,2048]{1,0:T(8,128)(2,1)} %param.19) | copy-start | bytes 3145732
  229.7 221.4 %all-gather.29.cloned.1.call-start = ((), (), s32[]{:S(2)}) async-start(), calls=%async_computation.21 | async-start | bytes 5242880 | tf_op jit(solution)/shard_map/all_gather | solution.py:232
  232.1 265.9 %all-gather.27.cloned.1.call-start = ((), (), s32[]{:S(2)}) async-start(), calls=%async_computation.19 | async-start | bytes 7077888 | tf_op jit(solution)/shard_map/all_gather | solution.py:148
  232.8 312.8 %all-gather.25.cloned.1.call-start = ((), (), s32[]{:S(2)}) async-start(), calls=%async_computation.18 | async-start | bytes 7077888 | tf_op jit(solution)/shard_map/all_gather | solution.py:147
  233.6 359.5 %all-gather.23.cloned.1.call-start = ((), (), s32[]{:S(2)}) async-start(), calls=%async_computation.17 | async-start | bytes 7077888 | tf_op jit(solution)/shard_map/all_gather | solution.py:146
  234.2 471.8 %reduce-scatter.16.cloned.1.call-start = ((), (), s32[]{:S(2)}) async-start(), calls=%async_computation.22 | async-start | bytes 5242880 | tf_op jit(solution)/shard_map/reduce_scatter | solution.py:241
  311.4 46.9 %collective-permute-start = (bf16[256,2048]{1,0:T(8,128)(2,1)}, bf16[256,2048]{1,0:T(8,128)(2,1)}, u32[]{:S(2)}, u32[]{:S(2)}) collective-permute-start(bf16[256,2048]{1,0:T(8,128)(2,1)} %get-tuple-element.225), channel_id=1, source_target_pairs={{0,1},{1,2},{2,3},{3,0},{4,5},{5,6},{6,7},{7,4},{8,9},{9,10},{10,1... | collective-permute-start | bytes 3145736 | tf_op jit(solution)/shard_map/ppermute | solution.py:194
  312.8 199.5 %collective-permute-start.1 = (bf16[256,2048]{1,0:T(8,128)(2,1)}, bf16[256,2048]{1,0:T(8,128)(2,1)}, u32[]{:S(2)}, u32[]{:S(2)}) collective-permute-start(bf16[256,2048]{1,0:T(8,128)(2,1)} %get-tuple-element.225), channel_id=1, source_target_pairs={{0,3},{1,0},{2,1},{3,2},{4,7},{5,4},{6,5},{7,6},{8,11},{9,8},{10,9... | collective-permute-start | bytes 3145736 | tf_op jit(solution)/shard_map/ppermute | solution.py:199
  358.3 156.3 %collective-permute-start.2 = (bf16[256,2048]{1,0:T(8,128)(2,1)}, bf16[256,2048]{1,0:T(8,128)(2,1)}, u32[]{:S(2)}, u32[]{:S(2)}) collective-permute-start(bf16[256,2048]{1,0:T(8,128)(2,1)} %collective-permute-done), channel_id=1, source_target_pairs={{0,1},{1,2},{2,3},{3,0},{4,5},{5,6},{6,7},{7,4},{8,9},{9,10},{10,1... | collective-permute-start | bytes 3145736 | tf_op jit(solution)/shard_map/ppermute | solution.py:194
  593.1 16.3 %copy-start.50 = (bf16[2048,1536]{1,0:T(8,128)(2,1)S(1)}, bf16[2048,1536]{1,0:T(8,128)(2,1)}, u32[]{:S(2)}) copy-start(bf16[2048,1536]{1,0:T(8,128)(2,1)} %all-gather.23.cloned.1.call-done) | copy-start | bytes 18874372
  609.4 8.9 copy-start.57
  609.4 8.9 copy-start.58
  609.4 8.9 copy-start.49
  629.0 156.4 %reduce-scatter.14.cloned.1.call-start = ((), (), s32[]{:S(2)}) async-start(), calls=%async_computation.20 | async-start | bytes 5242880 | tf_op jit(solution)/shard_map/reduce_scatter | solution.py:209
  640.2 231.7 %all-gather.31.cloned.1.call-start = ((), (), s32[]{:S(2)}) async-start(), calls=%async_computation.23 | async-start | bytes 5242880 | tf_op jit(solution)/shard_map/all_gather | solution.py:252
  790.5 160.4 %reduce-scatter.30.cloned.1.call-start = ((), (), s32[]{:S(2)}) async-start(), calls=%async_computation.30 | async-start | bytes 7077888 | tf_op jit(solution)/shard_map/reduce_scatter | solution.py:321
  802.0 198.8 %reduce-scatter.28.cloned.1.call-start = ((), (), s32[]{:S(2)}) async-start(), calls=%async_computation.29 | async-start | bytes 7077888 | tf_op jit(solution)/shard_map/reduce_scatter | solution.py:318
  814.1 252.1 %reduce-scatter.32.cloned.1.call-start = ((), (), s32[]{:S(2)}) async-start(), calls=%async_computation.31 | async-start | bytes 7077888 | tf_op jit(solution)/shard_map/reduce_scatter | solution.py:324
  828.7 51.8 %copy-start.15 = (bf16[2,1024,2,128]{3,1,2,0:T(8,128)(2,1)S(1)}, bf16[2,1024,2,128]{3,1,2,0:T(8,128)(2,1)}, u32[]{:S(2)}) copy-start(bf16[2,1024,2,128]{3,1,2,0:T(8,128)(2,1)} %copy-done.14) | copy-start | bytes 3145732
  828.7 276.6 %reduce-scatter.22.cloned.1.call-start = ((), (), s32[]{:S(2)}) async-start(), calls=%async_computation.26 | async-start | bytes 1179648 | tf_op jit(solution)/shard_map/reduce_scatter | solution.py:300
  909.9 5.2 copy-start.8
  930.9 214.1 %reduce-scatter.24.cloned.1.call-start = ((), (), s32[]{:S(2)}) async-start(), calls=%async_computation.27 | async-start | bytes 1179648 | tf_op jit(solution)/shard_map/reduce_scatter | solution.py:303
  931.4 258.0 %reduce-scatter.26.cloned.1.call-start = ((), (), s32[]{:S(2)}) async-start(), calls=%async_computation.28 | async-start | bytes 2359296 | tf_op jit(solution)/shard_map/reduce_scatter | solution.py:312
  937.8 296.4 %reduce-scatter.20.cloned.1.call-start = ((), (), s32[]{:S(2)}) async-start(), calls=%async_computation.25 | async-start | bytes 2359296 | tf_op jit(solution)/shard_map/reduce_scatter | solution.py:297
  941.0 372.3 %reduce-scatter.18.cloned.1.call-start = ((), (), s32[]{:S(2)}) async-start(), calls=%async_computation.24 | async-start | bytes 5242880 | tf_op jit(solution)/shard_map/reduce_scatter | solution.py:281
  950.8 362.5 %copy-start.1 = (bf16[256,2048]{1,0:T(8,128)(2,1)S(1)}, bf16[256,2048]{1,0:T(8,128)(2,1)}, u32[]{:S(2)}) copy-start(bf16[256,2048]{1,0:T(8,128)(2,1)} %param.19) | copy-start | bytes 3145732
  950.8 362.5 %copy-start.37 = (f32[8,1,256]{2,1,0:T(1,128)S(1)}, f32[8,1,256]{2,1,0:T(1,128)}, u32[]{:S(2)}) copy-start(f32[8,1,256]{2,1,0:T(1,128)} %copy-done.36) | copy-start | bytes 24580
  950.8 362.5 %copy-start.42 = (f32[256]{0:T(256)S(1)}, f32[256]{0:T(256)}, u32[]{:S(2)}) copy-start(f32[256]{0:T(256)} %copy-done.41) | copy-start | bytes 3076
  953.5 361.7 %copy-start.40 = (f32[2048]{0:T(1024)S(1)}, f32[2048]{0:T(1024)}, u32[]{:S(2)}) copy-start(f32[2048]{0:T(1024)} %get-tuple-element.171) | copy-start | bytes 24580
  953.5 393.4 %copy-start.17 = (f32[256,2048]{1,0:T(8,128)S(1)}, f32[256,2048]{1,0:T(8,128)}, u32[]{:S(2)}) copy-start(f32[256,2048]{1,0:T(8,128)} %get-tuple-element.223) | copy-start | bytes 6291460
  953.5 393.4 %copy-start.47 = (f32[256]{0:T(256)S(1)}, f32[256]{0:T(256)}, u32[]{:S(2)}) copy-start(f32[256]{0:T(256)} %get-tuple-element.254) | copy-start | bytes 3076
  (41 other events, 88.7 us)
Sparse Core Ops, SparseCore 0:
  10.0 30.6 all-gather.14
  42.5 23.5 all-gather.16
  68.0 23.4 all-gather.18
  93.6 80.7 all-gather.12
  176.1 26.7 all-gather.20
  229.8 75.3 reduce-scatter.11
  307.4 143.6 all-gather.28
  453.1 44.8 all-gather.26
  500.1 45.5 all-gather.24
  547.5 45.5 all-gather.22
  629.2 76.7 reduce-scatter.15
  708.1 77.2 reduce-scatter.13
  790.6 81.2 all-gather.30
  875.5 60.2 reduce-scatter.29
  939.0 61.7 reduce-scatter.27
  1004.4 61.7 reduce-scatter.31
  1069.2 36.0 reduce-scatter.21
  1108.9 36.0 reduce-scatter.23
  1148.2 41.2 reduce-scatter.25
  1193.0 41.2 reduce-scatter.19
  1236.5 76.7 reduce-scatter.17
